TPU v7x, 32 devices: a whole 2x2x4 slice. The times are simulated.
32 devices in a mesh: tile: 2 (over y), wave: 16 (over z, x, core).
Axes of the slice: x: 2, y: 2, z: 4, core: 2. Of those that a mesh axis runs over, the one named last changes fastest.
Arguments:
- frames: float32 [4, 1024, 4096], P(None, ('tile', 'wave')), parts along dimension 1, may hold values from -6 to 6
- inverse_var: float32 [4, 1024, 4096], P(None, ('tile', 'wave')), parts along dimension 1, may hold values from 0.2 to 240
- masked: int32 [4, 1024, 4096], P(None, ('tile', 'wave')), parts along dimension 1, may hold values 0 or 1
- psf_band: float32 [4, 1024, 16], P(None, ('tile', 'wave')), parts along dimension 1, may hold values from 0.02 to 0.2
- offsets: int32 [32], P(('tile', 'wave')), parts along dimension 0, may hold values from 18 to 31
- starts: int32 [32, 500], P(('tile', 'wave')), parts along dimension 0, may hold values from 0 to 3995, as said below
- profile: float32 [32, 12, 500], P(('tile', 'wave')), parts along dimension 0, may hold values from 0.05 to 0.5
- flux_start: float32 [1024, 500], P(('tile', 'wave')), parts along dimension 0, may hold values from -3 to 3
Outputs:
- solution: float32 [1024, 500], P(('tile', 'wave')), parts along dimension 0
- residual: float32 [1024, 500], P(('tile', 'wave')), parts along dimension 0
There are 2 independent parts, one for each index of `tile`. A program takes and returns all parts, laid end to end along the dimension named above; each array names one. Nothing has to cross between parts.
Inputs may be any that keep to these rules, and one draw needn't show every extreme that they name: In every slab, fiber k's trace starts at a column from 8k to 8k + 3, so the fibers lie in order, 8 columns apart give or take 3, and neighbouring profiles intersect.
All inputs are finite; a program needn't handle non-finite values. No bound on the sum of `masked` on one device may be relied on, other than what follows from the above.
Results may differ from a plain program's by a relative error of at most 0.0003.
Values sent between devices are 32-bit elements; how exact they have to be, the bound alone decides.
A program may use at most 64 MiB of HBM per device.

v0:
```python
import functools

import jax
import jax.numpy as jnp
from jax import lax
from jax.experimental import pallas as pl
from jax.experimental.pallas import tpu as pltpu
from jax.sharding import PartitionSpec as P

RIDGE = 0.2
REACH = 16
PITCH = 8
LANES = 128
SHIFTS = (6.0, 2.0)
F32, BF16 = jnp.float32, jnp.bfloat16
HIGH = lax.Precision.HIGHEST


def split(value):
    hi = value.astype(BF16)
    return hi, (value - hi.astype(F32)).astype(BF16)


def dot(a, b):
    return jnp.dot(a, b, preferred_element_type=F32)


def dot3(a, b):
    return dot(a[0], b[0]) + (dot(a[1], b[0]) + dot(a[0], b[1]))


def dot6(a, b):
    return jnp.dot(a, b, precision=HIGH, preferred_element_type=F32)


def total(value):
    return jnp.sum(value, keepdims=True)


def tri(d, o, y):
    wide = y.shape[1]
    return d * y + o * pltpu.roll(y, 1, 1) + pltpu.roll(o * y, wide - 1, 1)


def kernel(n, fr_hbm, iv_hbm, mk_hbm, band_ref, off_ref, st_ref, pr_ref, fl_ref, x_ref, r_ref,
           fr, iv, mk, pf, st, pk, g, fx, fbu, fbd, pku, pkd, fo, fiu, fid, vx, ra, da, oa, gown, gall,
           load, su, sd, ru, rd, gs, gr, *, chunks):
    expo, rows, cols = fr.shape
    fib = fl_ref.shape[1]
    wide = fx.shape[1]
    er = expo * rows
    span = cols // chunks
    me = lax.axis_index("wave")

    def loads(j):
        part = pl.ds(j * span, span)
        return [
            pltpu.make_async_copy(h.at[:, :, part], v.at[:, :, part], load.at[i, j])
            for i, (h, v) in enumerate(((iv_hbm, iv), (mk_hbm, mk), (fr_hbm, fr)))
        ]

    for j in range(chunks):
        for copy in loads(j):
            copy.start()

    fx[...] = jnp.zeros_like(fx)
    fbu[...] = jnp.zeros_like(fbu)
    fbd[...] = jnp.zeros_like(fbd)
    pku[...] = jnp.zeros_like(pku)
    pkd[...] = jnp.zeros_like(pkd)
    fiu[...] = jnp.zeros_like(fiu)
    fid[...] = jnp.zeros_like(fid)
    vx[...] = jnp.zeros_like(vx)

    barrier = pltpu.get_barrier_semaphore()

    @pl.loop(1, n)
    def _(d):
        pl.semaphore_signal(barrier, inc=1, device_id={"wave": lax.rem(me + d, n)},
                            device_id_type=pl.DeviceIdType.MESH)

    def pair(k, down_src, down_dst, up_src, up_dst):
        down = pltpu.make_async_remote_copy(
            src_ref=down_src, dst_ref=down_dst, send_sem=sd.at[k], recv_sem=rd.at[k],
            device_id={"wave": lax.rem(me + 1, n)}, device_id_type=pl.DeviceIdType.MESH)
        up = pltpu.make_async_remote_copy(
            src_ref=up_src, dst_ref=up_dst, send_sem=su.at[k], recv_sem=ru.at[k],
            device_id={"wave": lax.rem(me + n - 1, n)}, device_id_type=pl.DeviceIdType.MESH)
        return down, up

    def start(copies):
        @pl.when(me < n - 1)
        def _():
            copies[0].start()

        @pl.when(me > 0)
        def _():
            copies[1].start()

    def arrive(copies):
        @pl.when(me > 0)
        def _():
            copies[0].wait_recv()

        @pl.when(me < n - 1)
        def _():
            copies[1].wait_recv()

    def sent(copies):
        @pl.when(me < n - 1)
        def _():
            copies[0].wait_send()

        @pl.when(me > 0)
        def _():
            copies[1].wait_send()

    off = off_ref[0]
    lane = lax.broadcasted_iota(jnp.int32, (rows, LANES), 1)
    row = lax.broadcasted_iota(jnp.int32, (rows, LANES), 0)
    gap = lane - row - off
    band = band_ref[...]
    rm = jnp.zeros((expo, rows, LANES), F32)
    for j in range(band.shape[2]):
        rm = rm + jnp.where((gap == j)[None], band[:, :, j:j + 1], 0.0)
    own = rm.reshape(er, LANES)
    moved = jnp.where((row < REACH)[None], pltpu.roll(own, rows, 1).reshape(rm.shape),
                      pltpu.roll(own, LANES - rows, 1).reshape(rm.shape))
    pk[:, :, 2 * wide:] = moved
    ra[0:er, :] = own
    flux = fl_ref[...]
    fx[rows:2 * rows, 0:fib] = flux

    pf[...] = jnp.zeros_like(pf)
    st[...] = jnp.zeros_like(st)
    pf[4:4 + pr_ref.shape[1], 0:fib] = pr_ref[0]
    st[:, 0:fib] = st_ref[...] - PITCH * lax.broadcasted_iota(jnp.int32, (1, fib), 1)
    near = jnp.zeros((PITCH, wide), F32)
    far = jnp.zeros((PITCH, wide), F32)
    for shift in range(4):
        hit = jnp.broadcast_to(st[...], (PITCH, wide)) == shift
        near = near + jnp.where(hit, pf[4 - shift:12 - shift, :], 0.0)
        far = far + jnp.where(hit, pf[12 - shift:20 - shift, :], 0.0)
    near2, far2, both = near * near, far * far, near * pltpu.roll(far, 1, 1)

    pl.semaphore_wait(barrier, n - 1)
    flux_copies = pair(0, fl_ref.at[rows - REACH:rows], fbu, fl_ref.at[0:REACH], fbd)
    start(flux_copies)

    cube = (LANES, PITCH, LANES)
    depth = lax.broadcasted_iota(jnp.int32, cube, 0) - lax.broadcasted_iota(jnp.int32, cube, 2)
    on, after = depth == 0, depth == 1
    last = lax.broadcasted_iota(jnp.int32, (PITCH, LANES), 1) == LANES - 1

    def parts(value):
        hi = value.astype(BF16).astype(F32)
        return hi, value - hi

    def spread(a, b):
        rest = 0.0 if b is None else jnp.where(after, b[None], 0.0)
        return jnp.where(on, a[None], rest).reshape(LANES * PITCH, LANES).astype(BF16)

    def edge(b):
        top = jnp.where(last, b, 0.0)
        return jnp.concatenate([top, jnp.zeros((LANES - PITCH, LANES), F32)], axis=0).astype(BF16)

    for j in range(chunks):
        at = slice(j * LANES, (j + 1) * LANES)
        part = slice(j * span, (j + 1) * span)
        a2, b2, bo, an, bf = [parts(v[:, at]) for v in (near2, far2, both, near, far)]
        wrhs = [jnp.concatenate([spread(a2[i], b2[i]), spread(bo[i], None)], axis=1) for i in (0, 1)]
        frhs = [spread(an[i], bf[i]) for i in (0, 1)]
        for copy in loads(j):
            copy.wait()
        w = (iv[:, :, part] * (1.0 - mk[:, :, part].astype(F32))).reshape(er, span)
        wf = w * fr[:, :, part].reshape(er, span)
        w, wf = split(w), split(wf)
        got = dot3(w, wrhs)
        da[0:er, at] = got[:, 0:LANES]
        oa[0:er, at] = got[:, LANES:]
        g[:, at] = dot3(wf, frhs)
        if j > 0:
            prev = slice((j - 1) * LANES, j * LANES)
            b2, bf = [parts(v[:, prev]) for v in (far2, far)]
            da[0:er, prev] += dot3([v[:, 0:LANES] for v in w], [edge(v) for v in b2])
            g[:, prev] += dot3([v[:, 0:LANES] for v in wf], [edge(v) for v in bf])

    pk[:, :, 0:wide] = da[0:er, :].reshape(expo, rows, wide)
    pk[:, :, wide:2 * wide] = oa[0:er, :].reshape(expo, rows, wide)

    arrive(flux_copies)
    fx[rows - REACH:rows, 0:fib] = fbu[...]
    fx[2 * rows:2 * rows + REACH, 0:fib] = fbd[...]
    y = dot6(own, fx[...])
    own_t = own.T
    fo[0] = dot6(own_t, g[...] - tri(da[0:er, :], oa[0:er, :], y))
    fo[1] = dot6(own_t * own_t, da[0:er, :])
    fold_copies = pair(1, fo.at[:, 2 * rows:2 * rows + REACH], fiu, fo.at[:, rows - REACH:rows], fid)
    start(fold_copies)
    pack_copies = pair(2, pk.at[:, rows - REACH:rows], pku, pk.at[:, 0:REACH], pkd)
    start(pack_copies)

    arrive(fold_copies)
    res = fo[0, rows:2 * rows] - RIDGE * fx[rows:2 * rows, :] + jnp.concatenate([fiu[0], fid[0]], axis=0)
    diag = fo[1, rows:2 * rows] + RIDGE + jnp.concatenate([fiu[1], fid[1]], axis=0)
    inv = 1.0 / diag
    vs, us = [res * inv], []
    sums = [total(vs[0] * res)]
    v_copies = []
    ra_t = None
    for k in range(3):
        vx[k, rows:2 * rows] = vs[k]
        copies = pair(3 + k, vx.at[k, rows:2 * rows], vx.at[k, 0:rows],
                      vx.at[k, rows:2 * rows], vx.at[k, 2 * rows:3 * rows])
        start(copies)
        v_copies.append(copies)
        if k == 0:
            arrive(pack_copies)
            side = expo * REACH
            for i, ref in ((0, pku), (1, pkd)):
                place = slice(er + i * side, er + (i + 1) * side)
                da[place, :] = ref[:, :, 0:wide].reshape(side, wide)
                oa[place, :] = ref[:, :, wide:2 * wide].reshape(side, wide)
                ra[place, :] = ref[:, :, 2 * wide:].reshape(side, LANES)
            ra_t = ra[...].T[rows:2 * rows]
        arrive(copies)
        y = tri(da[...], oa[...], dot6(ra[...], vx[k]))
        us.append(dot6(ra_t, y) + RIDGE * vs[k])
        if k < 2:
            vs.append(us[k] * inv - SHIFTS[k] * vs[k])
            sums.append(total(vs[k + 1] * res))
    for i in range(3):
        for k in range(i, 3):
            sums.append(total(vs[i] * us[k]))

    spot = lax.broadcasted_iota(jnp.int32, (1, LANES), 1)
    mine = jnp.zeros((1, LANES), F32)
    for i, s in enumerate(sums):
        mine = jnp.where(spot == i, s, mine)
    gown[...] = mine
    gall[me] = mine

    def push(d):
        return pltpu.make_async_remote_copy(
            src_ref=gown, dst_ref=gall.at[me], send_sem=gs.at[d], recv_sem=gr.at[d],
            device_id={"wave": lax.rem(me + d, n)}, device_id_type=pl.DeviceIdType.MESH)

    @pl.loop(1, n)
    def _(d):
        push(d).start()

    @pl.loop(1, n)
    def _(d):
        push(d).wait_recv()

    whole = jnp.sum(gall[...], axis=0)
    b0, b1, b2, a00, a01, a02, a11, a12, a22 = [
        total(jnp.where(spot == i, whole, 0.0)) for i in range(9)]
    l10, l20 = a01 / a00, a02 / a00
    d1, e21 = a11 - l10 * a01, a12 - l20 * a01
    l21 = e21 / d1
    d2 = a22 - l20 * a02 - l21 * e21
    y1 = b1 - l10 * b0
    y2 = b2 - l20 * b0 - l21 * y1
    c2 = y2 / d2
    c1 = y1 / d1 - l21 * c2
    c0 = b0 / a00 - l10 * c1 - l20 * c2
    new_x = fx[rows:2 * rows, :] + (c0 * vs[0] + c1 * vs[1] + c2 * vs[2])
    new_r = res - (c0 * us[0] + c1 * us[1] + c2 * us[2])
    x_ref[...] = new_x[:, 0:fib]
    r_ref[...] = new_r[:, 0:fib]

    for copies in [flux_copies, fold_copies, pack_copies] + v_copies:
        sent(copies)

    @pl.loop(1, n)
    def _(d):
        push(d).wait_send()


def solution(mesh):
    n = mesh.shape["wave"]

    def local(frames, inverse_var, masked, psf_band, offsets, starts, profile, flux_start):
        expo, rows, cols = frames.shape
        fib = flux_start.shape[1]
        chunks = -(-fib // LANES)
        wide = chunks * LANES
        er, side = expo * rows, expo * REACH
        vmem, smem = pl.BlockSpec(memory_space=pltpu.VMEM), pl.BlockSpec(memory_space=pltpu.SMEM)
        far = pl.BlockSpec(memory_space=pl.ANY)
        out = jax.ShapeDtypeStruct(flux_start.shape, F32)
        dma = pltpu.SemaphoreType.DMA
        frame = (expo, rows, cols)
        return pl.pallas_call(
            functools.partial(kernel, n, chunks=chunks),
            out_shape=(out, out),
            in_specs=[far, far, far, vmem, smem, vmem, vmem, vmem],
            out_specs=(vmem, vmem),
            scratch_shapes=[
                pltpu.VMEM(frame, F32), pltpu.VMEM(frame, F32), pltpu.VMEM(frame, jnp.int32),
                pltpu.VMEM((24, wide), F32), pltpu.VMEM((1, wide), jnp.int32),
                pltpu.VMEM((expo, rows, 2 * wide + LANES), F32), pltpu.VMEM((er, wide), F32),
                pltpu.VMEM((LANES, wide), F32), pltpu.VMEM((REACH, fib), F32), pltpu.VMEM((REACH, fib), F32),
                pltpu.VMEM((expo, REACH, 2 * wide + LANES), F32), pltpu.VMEM((expo, REACH, 2 * wide + LANES), F32),
                pltpu.VMEM((2, LANES, wide), F32), pltpu.VMEM((2, REACH, wide), F32), pltpu.VMEM((2, REACH, wide), F32),
                pltpu.VMEM((3, LANES, wide), F32), pltpu.VMEM((er + 2 * side, LANES), F32),
                pltpu.VMEM((er + 2 * side, wide), F32), pltpu.VMEM((er + 2 * side, wide), F32),
                pltpu.VMEM((1, LANES), F32), pltpu.VMEM((n, 1, LANES), F32),
                dma((3, chunks)), dma((6,)), dma((6,)), dma((6,)), dma((6,)), dma((n,)), dma((n,)),
            ],
            compiler_params=pltpu.CompilerParams(
                collective_id=0, has_side_effects=True, vmem_limit_bytes=56 * 1024 * 1024),
        )(frames, inverse_var, masked, psf_band, offsets, starts, profile, flux_start)

    frame = P(None, ("tile", "wave"), None)
    flat = P(("tile", "wave"), None)
    return jax.shard_map(
        local, mesh=mesh,
        in_specs=(frame, frame, frame, frame, P(("tile", "wave")), flat, P(("tile", "wave"), None, None), flat),
        out_specs=(flat, flat), check_vma=False)
```

profile of v0, /device:TPU:0, one launch (start us, length us, event | category | flops | bytes accessed | tf_op | source)
XLA Modules:
  0.0 46.5 jit_solution(1906335791624461766)
XLA Ops:
  1.3 1.4 %copy.11.pr_ref = f32[1,12,500]{2,1,0:T(8,128)} copy(f32[1,12,500]{2,0,1:T(1,128)} %param.14) | data formatting | bytes 48000 | tf_op args[6]
  2.6 1.5 %copy.10.band_ref = f32[4,32,16]{2,1,0:T(8,128)} copy(f32[4,32,16]{1,2,0:T(8,128)} %param.11) | data formatting | bytes 16384 | tf_op args[3]
  4.1 39.4 %shard_map.95 = (f32[32,500]{1,0:T(8,128)}, f32[32,500]{1,0:T(8,128)}) custom-call(f32[4,32,4096]{2,1,0:T(8,128)} %fr_hbm.1, f32[4,32,4096]{2,1,0:T(8,128)} %iv_hbm.1, s32[4,32,4096]{2,1,0:T(8,128)} %mk_hbm.1, f32[4,32,16]{2,1,0:T(8,128)} %copy.10.band_ref, s32[1]{0:T(128)S(6)} %copy.14.off_ref, s32[1,500]{1,0:T(1,128)} %st_ref.1, ...), custom_call_target="tpu_custom_call" | custom-call | tf_op jit(solution)/shard_map/pallas_call | solution.py:295
  43.5 1.5 %copy.15 = f32[32,500]{1,0:T(8,128)} copy(f32[32,500]{1,0:T(8,128)} %get-tuple-element.4) | data formatting | bytes 128000
  45.0 1.5 %copy.16 = f32[32,500]{1,0:T(8,128)} copy(f32[32,500]{1,0:T(8,128)} %get-tuple-element.5) | data formatting | bytes 128000
where the time goes:
time: 46.9 us; the launch traced here: 46.5 us
  Pallas kernels  39.4 us (84%)
  local copies, waits for them, and re-layouts  5.77 us (12%)
  between operations  1.29 us (3%)
    pallas_call x1, Pallas kernels, local(): pl.pallas_call(functools.partial(kernel, n, chunks=chunks), out_shape=(ou...  39.4 us
    unnamed x4, local copies, waits for them, and re-layouts  5.77 us

commit v1 on v0

--- a/solution.py
+++ b/solution.py
@@ -16,19 +16,6 @@
 HIGH = lax.Precision.HIGHEST
 
 
-def split(value):
-    hi = value.astype(BF16)
-    return hi, (value - hi.astype(F32)).astype(BF16)
-
-
-def dot(a, b):
-    return jnp.dot(a, b, preferred_element_type=F32)
-
-
-def dot3(a, b):
-    return dot(a[0], b[0]) + (dot(a[1], b[0]) + dot(a[0], b[1]))
-
-
 def dot6(a, b):
     return jnp.dot(a, b, precision=HIGH, preferred_element_type=F32)
 
@@ -43,7 +30,7 @@
 
 
 def kernel(n, fr_hbm, iv_hbm, mk_hbm, band_ref, off_ref, st_ref, pr_ref, fl_ref, x_ref, r_ref,
-           fr, iv, mk, pf, st, pk, g, fx, fbu, fbd, pku, pkd, fo, fiu, fid, vx, ra, da, oa, gown, gall,
+           fr, iv, mk, pf, st, nr, fr2, acc, pk, rs, g, fx, fbu, fbd, pku, pkd, rsu, rsd, fo, fiu, fid, vx, ra, da, oa, gown, gall,
            load, su, sd, ru, rd, gs, gr, *, chunks):
     expo, rows, cols = fr.shape
     fib = fl_ref.shape[1]
@@ -59,7 +46,7 @@
             for i, (h, v) in enumerate(((iv_hbm, iv), (mk_hbm, mk), (fr_hbm, fr)))
         ]
 
-    for j in range(chunks):
+    for j in reversed(range(chunks)):
         for copy in loads(j):
             copy.start()
 
@@ -68,6 +55,8 @@
     fbd[...] = jnp.zeros_like(fbd)
     pku[...] = jnp.zeros_like(pku)
     pkd[...] = jnp.zeros_like(pkd)
+    rsu[...] = jnp.zeros_like(rsu)
+    rsd[...] = jnp.zeros_like(rsd)
     fiu[...] = jnp.zeros_like(fiu)
     fid[...] = jnp.zeros_like(fid)
     vx[...] = jnp.zeros_like(vx)
@@ -116,24 +105,25 @@
             copies[1].wait_send()
 
     off = off_ref[0]
-    lane = lax.broadcasted_iota(jnp.int32, (rows, LANES), 1)
-    row = lax.broadcasted_iota(jnp.int32, (rows, LANES), 0)
-    gap = lane - row - off
-    band = band_ref[...]
-    rm = jnp.zeros((expo, rows, LANES), F32)
-    for j in range(band.shape[2]):
-        rm = rm + jnp.where((gap == j)[None], band[:, :, j:j + 1], 0.0)
-    own = rm.reshape(er, LANES)
-    moved = jnp.where((row < REACH)[None], pltpu.roll(own, rows, 1).reshape(rm.shape),
-                      pltpu.roll(own, LANES - rows, 1).reshape(rm.shape))
-    pk[:, :, 2 * wide:] = moved
+    place = lax.broadcasted_iota(jnp.int32, (LANES, er), 0)
+    row = lax.broadcasted_iota(jnp.int32, (LANES, er), 1) % rows
+    gap = place - row - off
+    band = jnp.concatenate([band_ref[e] for e in range(expo)], axis=1)
+    own_t = jnp.zeros((LANES, er), F32)
+    for j in range(band.shape[0]):
+        own_t = own_t + jnp.where(gap == j, band[j:j + 1], 0.0)
+    own = own_t.T
     ra[0:er, :] = own
+    low = lax.broadcasted_iota(jnp.int32, (er, LANES), 0) % rows < REACH
+    moved = jnp.where(low, pltpu.roll(own, rows, 1), pltpu.roll(own, LANES - rows, 1))
+    rs[...] = moved.reshape(expo, rows, LANES)
     flux = fl_ref[...]
     fx[rows:2 * rows, 0:fib] = flux
 
     pf[...] = jnp.zeros_like(pf)
     st[...] = jnp.zeros_like(st)
-    pf[4:4 + pr_ref.shape[1], 0:fib] = pr_ref[0]
+    for p in range(pr_ref.shape[0]):
+        pf[4 + p:5 + p, 0:fib] = pr_ref[p]
     st[:, 0:fib] = st_ref[...] - PITCH * lax.broadcasted_iota(jnp.int32, (1, fib), 1)
     near = jnp.zeros((PITCH, wide), F32)
     far = jnp.zeros((PITCH, wide), F32)
@@ -141,65 +131,84 @@
         hit = jnp.broadcast_to(st[...], (PITCH, wide)) == shift
         near = near + jnp.where(hit, pf[4 - shift:12 - shift, :], 0.0)
         far = far + jnp.where(hit, pf[12 - shift:20 - shift, :], 0.0)
-    near2, far2, both = near * near, far * far, near * pltpu.roll(far, 1, 1)
+
+    def lay(ref, value):
+        ref[0:PITCH] = jnp.zeros((PITCH, LANES), F32)
+        for j in range(chunks):
+            block = value[:, j * LANES:(j + 1) * LANES]
+            ref[PITCH + j * LANES:PITCH + (j + 1) * LANES] = jnp.concatenate([block] * (LANES // PITCH), axis=0).T
+
+    lay(nr, near)
+    lay(fr2, far)
+    acc[...] = jnp.zeros_like(acc)
 
     pl.semaphore_wait(barrier, n - 1)
     flux_copies = pair(0, fl_ref.at[rows - REACH:rows], fbu, fl_ref.at[0:REACH], fbd)
     start(flux_copies)
 
-    cube = (LANES, PITCH, LANES)
-    depth = lax.broadcasted_iota(jnp.int32, cube, 0) - lax.broadcasted_iota(jnp.int32, cube, 2)
-    on, after = depth == 0, depth == 1
-    last = lax.broadcasted_iota(jnp.int32, (PITCH, LANES), 1) == LANES - 1
-
-    def parts(value):
+    row_copies = pair(2, rs.at[:, rows - REACH:rows], rsu, rs.at[:, 0:REACH], rsd)
+    start(row_copies)
+
+    tile = 2 * LANES
+    group = tile // PITCH
+    height = group + PITCH
+    line = lax.broadcasted_iota(jnp.int32, (height, tile), 0) - PITCH
+    mark = lax.broadcasted_iota(jnp.int32, (height, tile), 1) // PITCH
+    on, after = mark == line, mark == line + 1
+
+    def spread(a, b):
+        value = jnp.where(on, jnp.concatenate([a, a], axis=1), 0.0)
+        if b is not None:
+            value = jnp.where(after, jnp.concatenate([b, b], axis=1), value)
         hi = value.astype(BF16).astype(F32)
-        return hi, value - hi
-
-    def spread(a, b):
-        rest = 0.0 if b is None else jnp.where(after, b[None], 0.0)
-        return jnp.where(on, a[None], rest).reshape(LANES * PITCH, LANES).astype(BF16)
-
-    def edge(b):
-        top = jnp.where(last, b, 0.0)
-        return jnp.concatenate([top, jnp.zeros((LANES - PITCH, LANES), F32)], axis=0).astype(BF16)
-
-    for j in range(chunks):
-        at = slice(j * LANES, (j + 1) * LANES)
-        part = slice(j * span, (j + 1) * span)
-        a2, b2, bo, an, bf = [parts(v[:, at]) for v in (near2, far2, both, near, far)]
-        wrhs = [jnp.concatenate([spread(a2[i], b2[i]), spread(bo[i], None)], axis=1) for i in (0, 1)]
-        frhs = [spread(an[i], bf[i]) for i in (0, 1)]
+        return [hi, value - hi]
+
+    def narrow(blocks, weights):
+        left = jnp.concatenate(blocks, axis=0).astype(BF16)
+        hi = weights.astype(BF16)
+        right = jnp.concatenate([hi, (weights - hi.astype(F32)).astype(BF16)], axis=0)
+        out = lax.dot_general(left, right, (((1,), (1,)), ((), ())), preferred_element_type=F32)
+        half = len(blocks) * height // 2
+        return out[0:half, 0:er] + (out[0:half, er:] + out[half:, 0:er])
+
+    pack_copies = []
+    for j in reversed(range(chunks)):
         for copy in loads(j):
             copy.wait()
-        w = (iv[:, :, part] * (1.0 - mk[:, :, part].astype(F32))).reshape(er, span)
-        wf = w * fr[:, :, part].reshape(er, span)
-        w, wf = split(w), split(wf)
-        got = dot3(w, wrhs)
-        da[0:er, at] = got[:, 0:LANES]
-        oa[0:er, at] = got[:, LANES:]
-        g[:, at] = dot3(wf, frhs)
-        if j > 0:
-            prev = slice((j - 1) * LANES, j * LANES)
-            b2, bf = [parts(v[:, prev]) for v in (far2, far)]
-            da[0:er, prev] += dot3([v[:, 0:LANES] for v in w], [edge(v) for v in b2])
-            g[:, prev] += dot3([v[:, 0:LANES] for v in wf], [edge(v) for v in bf])
-
-    pk[:, :, 0:wide] = da[0:er, :].reshape(expo, rows, wide)
-    pk[:, :, wide:2 * wide] = oa[0:er, :].reshape(expo, rows, wide)
+        for t in reversed(range(j * span // tile, (j + 1) * span // tile)):
+            part = slice(t * tile, (t + 1) * tile)
+            at = slice(t * group, t * group + height)
+            an, bf = nr[at], fr2[at]
+            before = fr2[t * group + PITCH - 1:t * group + height - 1]
+            before = jnp.concatenate([jnp.zeros((PITCH, LANES), F32), before], axis=0)
+            w = (iv[:, :, part] * (1.0 - mk[:, :, part].astype(F32))).reshape(er, tile)
+            d_hi, d_lo = spread(an * an, bf * bf)
+            o_hi, o_lo = spread(an * before, None)
+            c_hi, c_lo = spread(an, bf)
+            got = narrow([d_hi, o_hi, d_lo, o_lo], w)
+            acc[0, at] += got[0:height]
+            acc[1, at] += got[height:]
+            acc[2, at] += narrow([c_hi, c_lo], w * fr[:, :, part].reshape(er, tile))
+        lanes = slice(j * LANES, (j + 1) * LANES)
+        done = slice(PITCH + j * LANES, PITCH + (j + 1) * LANES)
+        d, o = acc[0, done].T, acc[1, done].T
+        da[0:er, lanes] = d
+        oa[0:er, lanes] = o
+        g[:, lanes] = acc[2, done].T
+        pk[j, :, :, 0:LANES] = d.reshape(expo, rows, LANES)
+        pk[j, :, :, LANES:] = o.reshape(expo, rows, LANES)
+        copies = pair(6 + j, pk.at[j, :, rows - REACH:rows], pku.at[j], pk.at[j, :, 0:REACH], pkd.at[j])
+        start(copies)
+        pack_copies.append(copies)
 
     arrive(flux_copies)
     fx[rows - REACH:rows, 0:fib] = fbu[...]
     fx[2 * rows:2 * rows + REACH, 0:fib] = fbd[...]
     y = dot6(own, fx[...])
-    own_t = own.T
     fo[0] = dot6(own_t, g[...] - tri(da[0:er, :], oa[0:er, :], y))
     fo[1] = dot6(own_t * own_t, da[0:er, :])
     fold_copies = pair(1, fo.at[:, 2 * rows:2 * rows + REACH], fiu, fo.at[:, rows - REACH:rows], fid)
     start(fold_copies)
-    pack_copies = pair(2, pk.at[:, rows - REACH:rows], pku, pk.at[:, 0:REACH], pkd)
-    start(pack_copies)
-
     arrive(fold_copies)
     res = fo[0, rows:2 * rows] - RIDGE * fx[rows:2 * rows, :] + jnp.concatenate([fiu[0], fid[0]], axis=0)
     diag = fo[1, rows:2 * rows] + RIDGE + jnp.concatenate([fiu[1], fid[1]], axis=0)
@@ -215,13 +224,16 @@
         start(copies)
         v_copies.append(copies)
         if k == 0:
-            arrive(pack_copies)
+            for each in [row_copies] + pack_copies:
+                arrive(each)
             side = expo * REACH
-            for i, ref in ((0, pku), (1, pkd)):
+            for i, (ref, rowref) in enumerate(((pku, rsu), (pkd, rsd))):
                 place = slice(er + i * side, er + (i + 1) * side)
-                da[place, :] = ref[:, :, 0:wide].reshape(side, wide)
-                oa[place, :] = ref[:, :, wide:2 * wide].reshape(side, wide)
-                ra[place, :] = ref[:, :, 2 * wide:].reshape(side, LANES)
+                ra[place, :] = rowref[...].reshape(side, LANES)
+                for j in range(chunks):
+                    lanes = slice(j * LANES, (j + 1) * LANES)
+                    da[place, lanes] = ref[j, :, :, 0:LANES].reshape(side, LANES)
+                    oa[place, lanes] = ref[j, :, :, LANES:].reshape(side, LANES)
             ra_t = ra[...].T[rows:2 * rows]
         arrive(copies)
         y = tri(da[...], oa[...], dot6(ra[...], vx[k]))
@@ -270,12 +282,17 @@
     x_ref[...] = new_x[:, 0:fib]
     r_ref[...] = new_r[:, 0:fib]
 
-    for copies in [flux_copies, fold_copies, pack_copies] + v_copies:
+    for copies in [flux_copies, fold_copies, row_copies] + pack_copies + v_copies:
         sent(copies)
 
     @pl.loop(1, n)
     def _(d):
         push(d).wait_send()
+
+
+def hand_over(x_ref, r_ref, x_out, r_out):
+    x_out[...] = x_ref[...]
+    r_out[...] = r_ref[...]
 
 
 def solution(mesh):
@@ -292,7 +309,7 @@
         out = jax.ShapeDtypeStruct(flux_start.shape, F32)
         dma = pltpu.SemaphoreType.DMA
         frame = (expo, rows, cols)
-        return pl.pallas_call(
+        found = pl.pallas_call(
             functools.partial(kernel, n, chunks=chunks),
             out_shape=(out, out),
             in_specs=[far, far, far, vmem, smem, vmem, vmem, vmem],
@@ -300,18 +317,23 @@
             scratch_shapes=[
                 pltpu.VMEM(frame, F32), pltpu.VMEM(frame, F32), pltpu.VMEM(frame, jnp.int32),
                 pltpu.VMEM((24, wide), F32), pltpu.VMEM((1, wide), jnp.int32),
-                pltpu.VMEM((expo, rows, 2 * wide + LANES), F32), pltpu.VMEM((er, wide), F32),
+                pltpu.VMEM((wide + PITCH, LANES), F32), pltpu.VMEM((wide + PITCH, LANES), F32),
+                pltpu.VMEM((3, wide + PITCH, er), F32), pltpu.VMEM((chunks, expo, rows, 2 * LANES), F32),
+                pltpu.VMEM((expo, rows, LANES), F32), pltpu.VMEM((er, wide), F32),
                 pltpu.VMEM((LANES, wide), F32), pltpu.VMEM((REACH, fib), F32), pltpu.VMEM((REACH, fib), F32),
-                pltpu.VMEM((expo, REACH, 2 * wide + LANES), F32), pltpu.VMEM((expo, REACH, 2 * wide + LANES), F32),
+                pltpu.VMEM((chunks, expo, REACH, 2 * LANES), F32), pltpu.VMEM((chunks, expo, REACH, 2 * LANES), F32),
+                pltpu.VMEM((expo, REACH, LANES), F32), pltpu.VMEM((expo, REACH, LANES), F32),
                 pltpu.VMEM((2, LANES, wide), F32), pltpu.VMEM((2, REACH, wide), F32), pltpu.VMEM((2, REACH, wide), F32),
                 pltpu.VMEM((3, LANES, wide), F32), pltpu.VMEM((er + 2 * side, LANES), F32),
                 pltpu.VMEM((er + 2 * side, wide), F32), pltpu.VMEM((er + 2 * side, wide), F32),
                 pltpu.VMEM((1, LANES), F32), pltpu.VMEM((n, 1, LANES), F32),
-                dma((3, chunks)), dma((6,)), dma((6,)), dma((6,)), dma((6,)), dma((n,)), dma((n,)),
+                dma((3, chunks)), *[dma((6 + chunks,))] * 4, dma((n,)), dma((n,)),
             ],
             compiler_params=pltpu.CompilerParams(
                 collective_id=0, has_side_effects=True, vmem_limit_bytes=56 * 1024 * 1024),
-        )(frames, inverse_var, masked, psf_band, offsets, starts, profile, flux_start)
+        )(frames, inverse_var, masked, jnp.swapaxes(psf_band, 1, 2), offsets, starts,
+          jnp.swapaxes(profile, 0, 1), flux_start)
+        return pl.pallas_call(hand_over, out_shape=(out, out), in_specs=[vmem, vmem], out_specs=(vmem, vmem))(*found)
 
     frame = P(None, ("tile", "wave"), None)
     flat = P(("tile", "wave"), None)

time: 46.9 us -> 38.1 us (0.81)
  local copies, waits for them, and re-layouts: 5.77 us -> 0 us
  Pallas kernels: 39.4 us -> 36.6 us
    unnamed x4 -> x0, local copies, waits for them, and re-layouts: 5.77 us -> none
    pallas_call x1, Pallas kernels: 39.4 us -> 35 us  [local(): pl.pallas_call(functools.partial(kernel, n, chunks=chunks), out_shape=(ou...]
    pallas_call x0 -> x1, Pallas kernels: none -> 1.53 us  [local(): pl.pallas_call(hand_over, out_shape=(out, out), in_specs=[vmem, vmem], ou...]
where the time goes in v1:
time: 38.1 us; the launch traced here: 37.9 us
  Pallas kernels  36.6 us (96%)
  between operations  1.29 us (3%)
    pallas_call x1, Pallas kernels, local(): pl.pallas_call(functools.partial(kernel, n, chunks=chunks), out_shape=(ou...  35 us
    pallas_call x1, Pallas kernels, local(): pl.pallas_call(hand_over, out_shape=(out, out), in_specs=[vmem, vmem], ou...  1.53 us

profile of v1, /device:TPU:0, one launch (start us, length us, event | category | flops | bytes accessed | tf_op | source)
XLA Modules:
  0.0 37.9 jit_solution(4707026626992864829)
XLA Ops:
  1.3 35.0 %shard_map.95 = (f32[32,500]{1,0:T(8,128)}, f32[32,500]{1,0:T(8,128)}) custom-call(f32[4,32,4096]{2,1,0:T(8,128)} %fr_hbm.1, f32[4,32,4096]{2,1,0:T(8,128)} %iv_hbm.1, s32[4,32,4096]{2,1,0:T(8,128)} %mk_hbm.1, f32[4,16,32]{2,1,0:T(8,128)} %bitcast.2, s32[1]{0:T(128)S(6)} %copy.10.off_ref, s32[1,500]{1,0:T(1,128)} %st_ref.1, f32[12,1,500]{2,1,0:T(1,128)} %bitcast.3, ...), custom_call_target="tpu_custom_call" | custom-call | tf_op jit(solution)/shard_map/pallas_call | solution.py:312
  36.3 1.5 %shard_map.96 = (f32[32,500]{1,0:T(8,128)}, f32[32,500]{1,0:T(8,128)}) custom-call(f32[32,500]{1,0:T(8,128)} %get-tuple-element.4.x_ref, f32[32,500]{1,0:T(8,128)} %get-tuple-element.5.r_ref), custom_call_target="tpu_custom_call" | custom-call | tf_op jit(solution)/shard_map/pallas_call | solution.py:336

commit v2 on v1

--- a/solution.py
+++ b/solution.py
@@ -198,7 +198,8 @@
         pk[j, :, :, 0:LANES] = d.reshape(expo, rows, LANES)
         pk[j, :, :, LANES:] = o.reshape(expo, rows, LANES)
         copies = pair(6 + j, pk.at[j, :, rows - REACH:rows], pku.at[j], pk.at[j, :, 0:REACH], pkd.at[j])
-        start(copies)
+        if j > 0:
+            start(copies)
         pack_copies.append(copies)
 
     arrive(flux_copies)
@@ -209,6 +210,7 @@
     fo[1] = dot6(own_t * own_t, da[0:er, :])
     fold_copies = pair(1, fo.at[:, 2 * rows:2 * rows + REACH], fiu, fo.at[:, rows - REACH:rows], fid)
     start(fold_copies)
+    start(pack_copies[-1])
     arrive(fold_copies)
     res = fo[0, rows:2 * rows] - RIDGE * fx[rows:2 * rows, :] + jnp.concatenate([fiu[0], fid[0]], axis=0)
     diag = fo[1, rows:2 * rows] + RIDGE + jnp.concatenate([fiu[1], fid[1]], axis=0)
@@ -236,14 +238,17 @@
                     oa[place, lanes] = ref[j, :, :, LANES:].reshape(side, LANES)
             ra_t = ra[...].T[rows:2 * rows]
         arrive(copies)
-        y = tri(da[...], oa[...], dot6(ra[...], vx[k]))
-        us.append(dot6(ra_t, y) + RIDGE * vs[k])
+        image = dot6(ra[...], vx[k])
+        y = tri(da[...], oa[...], image)
         if k < 2:
+            us.append(dot6(ra_t, y) + RIDGE * vs[k])
             vs.append(us[k] * inv - SHIFTS[k] * vs[k])
             sums.append(total(vs[k + 1] * res))
-    for i in range(3):
-        for k in range(i, 3):
+    for i in range(2):
+        for k in range(i, 2):
             sums.append(total(vs[i] * us[k]))
+        sums.append(total(us[i] * vs[2]))
+    sums.append(total(image[0:er] * y[0:er]) + RIDGE * total(vs[2] * vs[2]))
 
     spot = lax.broadcasted_iota(jnp.int32, (1, LANES), 1)
     mine = jnp.zeros((1, LANES), F32)
@@ -260,6 +265,8 @@
     @pl.loop(1, n)
     def _(d):
         push(d).start()
+
+    us.append(dot6(ra_t, y) + RIDGE * vs[2])
 
     @pl.loop(1, n)
     def _(d):

time: 38.1 us -> 36.3 us (0.953)
  Pallas kernels: 36.6 us -> 34.8 us
    pallas_call x1, Pallas kernels: 35 us -> 33.2 us  [local(): pl.pallas_call(functools.partial(kernel, n, chunks=chunks), out_shape=(ou...]
where the time goes in v2:
time: 36.3 us; the launch traced here: 36 us
  Pallas kernels  34.8 us (96%)
  between operations  1.29 us (4%)
    pallas_call x1, Pallas kernels, local(): pl.pallas_call(functools.partial(kernel, n, chunks=chunks), out_shape=(ou...  33.2 us
    pallas_call x1, Pallas kernels, local(): pl.pallas_call(hand_over, out_shape=(out, out), in_specs=[vmem, vmem], ou...  1.53 us

profile of v2, /device:TPU:0, one launch (start us, length us, event | category | flops | bytes accessed | tf_op | source)
XLA Modules:
  0.0 36.0 jit_solution(5034198576650107376)
XLA Ops:
  1.3 33.2 %shard_map.95 = (f32[32,500]{1,0:T(8,128)}, f32[32,500]{1,0:T(8,128)}) custom-call(f32[4,32,4096]{2,1,0:T(8,128)} %fr_hbm.1, f32[4,32,4096]{2,1,0:T(8,128)} %iv_hbm.1, s32[4,32,4096]{2,1,0:T(8,128)} %mk_hbm.1, f32[4,16,32]{2,1,0:T(8,128)} %bitcast.2, s32[1]{0:T(128)S(6)} %copy.10.off_ref, s32[1,500]{1,0:T(1,128)} %st_ref.1, f32[12,1,500]{2,1,0:T(1,128)} %bitcast.3, ...), custom_call_target="tpu_custom_call" | custom-call | tf_op jit(solution)/shard_map/pallas_call | solution.py:319
  34.5 1.5 %shard_map.96 = (f32[32,500]{1,0:T(8,128)}, f32[32,500]{1,0:T(8,128)}) custom-call(f32[32,500]{1,0:T(8,128)} %get-tuple-element.4.x_ref, f32[32,500]{1,0:T(8,128)} %get-tuple-element.5.r_ref), custom_call_target="tpu_custom_call" | custom-call | tf_op jit(solution)/shard_map/pallas_call | solution.py:343

commit v3 on v2

--- a/solution.py
+++ b/solution.py
@@ -18,6 +18,19 @@
 
 def dot6(a, b):
     return jnp.dot(a, b, precision=HIGH, preferred_element_type=F32)
+
+
+def dot(a, b):
+    return jnp.dot(a, b, preferred_element_type=F32)
+
+
+def split(value):
+    hi = value.astype(BF16)
+    return hi, (value - hi.astype(F32)).astype(BF16)
+
+
+def dot3(a, b):
+    return dot(a[0], b[0]) + (dot(a[1], b[0]) + dot(a[0], b[1]))
 
 
 def total(value):
@@ -236,12 +249,12 @@
                     lanes = slice(j * LANES, (j + 1) * LANES)
                     da[place, lanes] = ref[j, :, :, 0:LANES].reshape(side, LANES)
                     oa[place, lanes] = ref[j, :, :, LANES:].reshape(side, LANES)
-            ra_t = ra[...].T[rows:2 * rows]
+            ra_s, ra_t = split(ra[...]), split(ra[...].T[rows:2 * rows])
         arrive(copies)
-        image = dot6(ra[...], vx[k])
+        image = dot3(ra_s, split(vx[k]))
         y = tri(da[...], oa[...], image)
         if k < 2:
-            us.append(dot6(ra_t, y) + RIDGE * vs[k])
+            us.append(dot3(ra_t, split(y)) + RIDGE * vs[k])
             vs.append(us[k] * inv - SHIFTS[k] * vs[k])
             sums.append(total(vs[k + 1] * res))
     for i in range(2):
@@ -266,7 +279,7 @@
     def _(d):
         push(d).start()
 
-    us.append(dot6(ra_t, y) + RIDGE * vs[2])
+    us.append(dot3(ra_t, split(y)) + RIDGE * vs[2])
 
     @pl.loop(1, n)
     def _(d):

time: 36.3 us -> 35.4 us (0.975)
  Pallas kernels: 34.8 us -> 33.9 us
    pallas_call x1, Pallas kernels: 33.2 us -> 32.4 us  [local(): pl.pallas_call(functools.partial(kernel, n, chunks=chunks), out_shape=(ou...]
where the time goes in v3:
time: 35.4 us; the launch traced here: 35.2 us
  Pallas kernels  33.9 us (96%)
  between operations  1.29 us (4%)
    pallas_call x1, Pallas kernels, local(): pl.pallas_call(functools.partial(kernel, n, chunks=chunks), out_shape=(ou...  32.4 us
    pallas_call x1, Pallas kernels, local(): pl.pallas_call(hand_over, out_shape=(out, out), in_specs=[vmem, vmem], ou...  1.53 us

profile of v3, /device:TPU:0, one launch (start us, length us, event | category | flops | bytes accessed | tf_op | source)
XLA Modules:
  0.0 35.2 jit_solution(13127829180373368064)
XLA Ops:
  1.3 32.4 %shard_map.95 = (f32[32,500]{1,0:T(8,128)}, f32[32,500]{1,0:T(8,128)}) custom-call(f32[4,32,4096]{2,1,0:T(8,128)} %fr_hbm.1, f32[4,32,4096]{2,1,0:T(8,128)} %iv_hbm.1, s32[4,32,4096]{2,1,0:T(8,128)} %mk_hbm.1, f32[4,16,32]{2,1,0:T(8,128)} %bitcast.2, s32[1]{0:T(128)S(6)} %copy.10.off_ref, s32[1,500]{1,0:T(1,128)} %st_ref.1, f32[12,1,500]{2,1,0:T(1,128)} %bitcast.3, ...), custom_call_target="tpu_custom_call" | custom-call | tf_op jit(solution)/shard_map/pallas_call | solution.py:332
  33.7 1.5 %shard_map.96 = (f32[32,500]{1,0:T(8,128)}, f32[32,500]{1,0:T(8,128)}) custom-call(f32[32,500]{1,0:T(8,128)} %get-tuple-element.4.x_ref, f32[32,500]{1,0:T(8,128)} %get-tuple-element.5.r_ref), custom_call_target="tpu_custom_call" | custom-call | tf_op jit(solution)/shard_map/pallas_call | solution.py:356
